TPU v7x, 512 devices: a whole 4x8x8 slice. The times are simulated.
512 devices in a mesh: lon: 64 (over z_lo, y, core), plane: 8 (over z_hi, x).
Axes of the slice: x: 4, y: 8, z: 8 (z_hi: 2, z_lo: 4; z = z_hi * 4 + z_lo), core: 2. Of those that a mesh axis runs over, the one named last changes fastest.
Arguments:
- potential: float32 [8, 256, 16384], P('plane', None, 'lon'), may hold values from -0.6 to 0.6
- lens_weight: float32 [8, 8], P('plane'), may hold values from 0.1 to 0.3
- cycle_shift: int32 [2, 256], replicated, may hold values from -3 to 2
- cycle_weight: int32 [2, 256], replicated, may hold values from 0 to 16
- cycle_scale: float32 [256], replicated, may hold values from 1 to 2
Outputs:
- displacement: float32 [8, 2, 256, 16384], P('plane', None, None, 'lon')
- jacobian: float32 [8, 4, 256, 16384], P('plane', None, None, 'lon')
All inputs are finite; a program needn't handle non-finite values.
Results may differ from a plain program's by a relative error of at most 0.00002.
Values sent between devices are 32-bit elements; how exact they have to be, the bound alone decides.
No kernel may reach another device: no remote copies, remote signals or barrier semaphores. Data moves between devices by JAX's collectives and lax.ppermute only.
A program may use at most 64 MiB of HBM per device.

v0:
```python
import jax
import jax.numpy as jnp
from jax import lax
from jax.sharding import PartitionSpec as P

HALO = 4


def shifted(value, axis, steps):
    count = lax.axis_size(axis)
    pairs = [(source, (source + steps) % count) for source in range(count)]
    return lax.ppermute(value, axis, pairs)


def extended(block, sides, width):
    for axis, dim in sides:
        count = lax.axis_size(axis)
        forward = [(i, i + 1) for i in range(count - 1)]
        forward.append((count - 1, 0))
        backward = [(target, source) for source, target in forward]
        low = lax.ppermute(
            lax.slice_in_dim(block, block.shape[dim] - width, None, axis=dim), axis, forward
        )
        high = lax.ppermute(lax.slice_in_dim(block, 0, width, axis=dim), axis, backward)
        block = jnp.concatenate([low, block, high], axis=dim)
    return block


def from_root(shard, axis, root):
    mine = lax.axis_index(axis) == root
    return lax.psum(jnp.where(mine, shard, jnp.zeros_like(shard)), axis)


def pick_cycle(row_block, shifts, offset, width):
    result = jnp.zeros((row_block.shape[0], width), jnp.float32)
    for delta in range(-3, 3):
        start = HALO + delta + offset
        result = jnp.where(shifts[:, None] == delta, row_block[:, start : start + width], result)
    return result


def cycle_value(row_block, shifts, weights, offset, width):
    frac = weights.astype(jnp.float32)[:, None] / 16.0
    first = pick_cycle(row_block, shifts, offset, width)
    second = pick_cycle(row_block, shifts, offset + 1, width)
    return (1.0 - frac) * first + frac * second


def derivatives(padded, cycle_shift, cycle_weight, cycle_scale):
    width = padded.shape[1] - 2 * HALO
    north_rows = padded[:-2]
    south_rows = padded[2:]
    middle = padded[1:-1]
    north = [
        cycle_value(north_rows, cycle_shift[0], cycle_weight[0], offset, width)
        for offset in (-1, 0, 1)
    ]
    south = [
        cycle_value(south_rows, cycle_shift[1], cycle_weight[1], offset, width)
        for offset in (-1, 0, 1)
    ]
    center = [middle[:, HALO + offset : HALO + offset + width] for offset in (-1, 0, 1)]
    metric = cycle_scale[:, None]
    alpha_t = 0.5 * (south[1] - north[1])
    alpha_p = 0.5 * metric * (center[2] - center[0])
    shear_tt = south[1] - 2.0 * center[1] + north[1]
    shear_pp = metric * metric * (center[2] - 2.0 * center[1] + center[0])
    shear_tp = 0.25 * metric * (south[2] - south[0] - north[2] + north[0])
    return (alpha_t, alpha_p, shear_tt, shear_pp, shear_tp)


def advance(state, fields, gain):
    disp_t, disp_p, a_zz, a_zo, a_oz, a_oo = state
    alpha_t, alpha_p, shear_tt, shear_pp, shear_tp = fields
    new_t = disp_t - gain * (alpha_t + shear_tt * disp_t + shear_tp * disp_p)
    new_p = disp_p - gain * (alpha_p + shear_tp * disp_t + shear_pp * disp_p)
    b_zz = a_zz - gain * (shear_tt * a_zz + shear_tp * a_oz)
    b_zo = a_zo - gain * (shear_tt * a_zo + shear_tp * a_oo)
    b_oz = a_oz - gain * (shear_tp * a_zz + shear_pp * a_oz)
    b_oo = a_oo - gain * (shear_tp * a_zo + shear_pp * a_oo)
    return (new_t, new_p, b_zz, b_zo, b_oz, b_oo)


def pad_rows(tile):
    return jnp.pad(tile, ((1, 1), (0, 0)))


def per_device(potential, lens_weight, cycle_shift, cycle_weight, cycle_scale):
    planes = lax.axis_size("plane")
    lon_count = lax.axis_size("lon")
    by_tiles = lon_count - lon_count // 4
    rows_count = potential.shape[1]
    width = potential.shape[2]
    gains = lens_weight[0]
    zeros = jnp.zeros((rows_count, width), jnp.float32)
    ones = jnp.ones((rows_count, width), jnp.float32)
    state = (zeros, zeros, ones, zeros, zeros, ones)
    for plane_k in range(planes):
        turned = shifted(from_root(potential, "plane", plane_k), "lon", by_tiles)
        sky_tile = extended(turned, (("lon", 2),), HALO)[0]
        fields = derivatives(pad_rows(sky_tile), cycle_shift, cycle_weight, cycle_scale)
        state = advance(state, fields, gains[plane_k])
    displacement = jnp.stack(state[0:2])[None]
    jacobian = jnp.stack(state[2:6])[None]
    return (displacement, jacobian)


def solution(mesh):
    in_specs = (P("plane", None, "lon"), P("plane", None), P(), P(), P())
    out_specs = (P("plane", None, None, "lon"), P("plane", None, None, "lon"))
    return jax.shard_map(
        per_device, mesh=mesh, in_specs=in_specs, out_specs=out_specs, check_vma=False
    )
```

profile of v0, /device:TPU:6, one launch (start us, length us, event | category | flops | bytes accessed | tf_op | source)
XLA Modules:
  0.0 324.3 jit_solution(139829288068550160)
XLA Ops:
  7.2 2.3 broadcast_select_fusion
  10.9 149.9 %all-reduce.11.cloned.1.call-done = (f32[1,256,256]{2,1,0:T(8,128)}, f32[1,256,256]{2,1,0:T(8,128)}, f32[1,256,256]{2,1,0:T(8,128)}, f32[1,256,256]{2,1,0:T(8,12...) async-done(((f32[1,256,256]{2,1,0:T(8,128)}, f32[1,256,256]{2,1,0:T(8,128)}, f32[1,256,256]{2,1,0:T(8,128)}, ...) | async-done | bytes 2097168 | tf_op jit(solution)/shard_map/psum | solution.py:31
  168.0 6.8 %collective-permute-start.9 = (f32[1,256,256]{2,1,0:T(8,128)}, f32[1,256,256]{2,1,0:T(8,128)S(1)}, u32[]{:S(2)}, u32[]{:S(2)}) collective-permute-start(f32[1,256,256]{2,1,0:T(8,128)} %get-tuple-element.17), channel_id=1, source_target_pairs={{0,384},{8,392},{16,400},{24,408},{32,416},{40,424},{48,432},{56,4... | collective-permute-start | bytes 786440 | tf_op jit(solution)/shard_map/ppermute | solution.py:12
  176.8 2.1 collective-permute-start.15
  179.0 2.5 collective-permute-start.18
  183.3 4.7 %collective-permute-start.21 = (f32[1,256,256]{2,1,0:T(8,128)S(1)}, f32[1,256,256]{2,1,0:T(8,128)S(1)}, u32[]{:S(2)}, u32[]{:S(2)}) collective-permute-start(f32[1,256,256]{2,1,0:T(8,128)S(1)} %copy-done.4), channel_id=1, source_target_pairs={{0,384},{8,392},{16,400},{24,408},{32,416},{40,424},{48,432},{56,4... | collective-permute-start | bytes 786440 | tf_op jit(solution)/shard_map/ppermute | solution.py:12
  190.9 3.6 %collective-permute-done.12 = f32[1,256,256]{2,1,0:T(8,128)S(1)} collective-permute-done((f32[1,256,256]{2,1,0:T(8,128)}, f32[1,256,256]{2,1,0:T(8,128)S(1)}, u32[]{:S(2)}, u32[]{:S(2)}) %collective-permute-start.12) | collective-permute-done | bytes 262176 | tf_op jit(solution)/shard_map/ppermute | solution.py:12
  194.5 4.0 %collective-permute-start.2 = (f32[1,256,4]{2,1,0:T(8,128)S(1)}, f32[1,256,4]{2,1,0:T(8,128)S(1)}, u32[]{:S(2)}, u32[]{:S(2)}) collective-permute-start(f32[1,256,4]{2,1,0:T(8,128)S(1)} %get-tuple-element.114), channel_id=1, source_target_pairs={{8,0},{16,8},{24,16},{32,24},{40,32},{48,40},{56,48},{64,56},{72,6... | collective-permute-start | bytes 12296 | tf_op jit(solution)/shard_map/ppermute | solution.py:24
  198.6 3.0 collective-permute-done.15
  203.5 4.5 %collective-permute-done.18 = f32[1,256,256]{2,1,0:T(8,128)S(1)} collective-permute-done((f32[1,256,256]{2,1,0:T(8,128)S(1)}, f32[1,256,256]{2,1,0:T(8,128)S(1)}, u32[]{:S(2)}, u32[]{:S(2)}) %collective-permute-start.18) | collective-permute-done | bytes 262176 | tf_op jit(solution)/shard_map/ppermute | solution.py:12
  208.0 3.1 collective-permute-start.5
  214.2 7.5 %collective-permute-start.8 = (f32[1,256,4]{2,1,0:T(8,128)S(1)}, f32[1,256,4]{2,1,0:T(8,128)S(1)}, u32[]{:S(2)}, u32[]{:S(2)}) collective-permute-start(f32[1,256,4]{2,1,0:T(8,128)S(1)} %get-tuple-element.112), channel_id=1, source_target_pairs={{8,0},{16,8},{24,16},{32,24},{40,32},{48,40},{56,48},{64,56},{72,6... | collective-permute-start | bytes 12296 | tf_op jit(solution)/shard_map/ppermute | solution.py:24
  221.8 1.9 collective-permute-start.10
  224.0 7.5 %collective-permute-start.11 = (f32[1,256,4]{2,1,0:T(8,128)S(1)}, f32[1,256,4]{2,1,0:T(8,128)S(1)}, u32[]{:S(2)}, u32[]{:S(2)}) collective-permute-start(f32[1,256,4]{2,1,0:T(8,128)S(1)} %get-tuple-element.118), channel_id=1, source_target_pairs={{8,0},{16,8},{24,16},{32,24},{40,32},{48,40},{56,48},{64,56},{72,6... | collective-permute-start | bytes 12296 | tf_op jit(solution)/shard_map/ppermute | solution.py:24
  231.5 1.9 collective-permute-start.13
  233.7 6.8 %multiply_subtract_fusion.25 = (f32[256,256]{1,0:T(8,128)S(1)}, f32[256,256]{1,0:T(8,128)S(1)}, f32[256,256]{1,0:T(8,128)S(1)}, f32[256,256]{1,0:T(8,128)S(1)}, ...) fusion(f32[]{:T(128)} %bitcast.4, f32[]{:T(128)} %bitcast, ...), kind=kLoop, calls=%fused_computation.47 | loop fusion | flops 13762560 | bytes 4206600 | tf_op jit(solution)/shard_map/sub | solution.py:77
  243.9 7.5 %collective-permute-start.14 = (f32[1,256,4]{2,1,0:T(8,128)S(1)}, f32[1,256,4]{2,1,0:T(8,128)S(1)}, u32[]{:S(2)}, u32[]{:S(2)}) collective-permute-start(f32[1,256,4]{2,1,0:T(8,128)S(1)} %get-tuple-element.110), channel_id=1, source_target_pairs={{8,0},{16,8},{24,16},{32,24},{40,32},{48,40},{56,48},{64,56},{72,6... | collective-permute-start | bytes 12296 | tf_op jit(solution)/shard_map/ppermute | solution.py:24
  253.6 7.5 %collective-permute-start.17 = (f32[1,256,4]{2,1,0:T(8,128)S(1)}, f32[1,256,4]{2,1,0:T(8,128)S(1)}, u32[]{:S(2)}, u32[]{:S(2)}) collective-permute-start(f32[1,256,4]{2,1,0:T(8,128)S(1)} %get-tuple-element.120), channel_id=1, source_target_pairs={{8,0},{16,8},{24,16},{32,24},{40,32},{48,40},{56,48},{64,56},{72,6... | collective-permute-start | bytes 12296 | tf_op jit(solution)/shard_map/ppermute | solution.py:24
  263.3 6.9 %multiply_subtract_fusion.21 = (f32[256,256]{1,0:T(8,128)S(1)}, f32[256,256]{1,0:T(8,128)S(1)}, f32[256,256]{1,0:T(8,128)S(1)}, f32[256,256]{1,0:T(8,128)S(1)}, ...) fusion(f32[]{:T(128)} %bitcast.8, ...), kind=kLoop, calls=%fused_computation.43 | loop fusion | flops 13893632 | bytes 4993032 | tf_op jit(solution)/shard_map/sub | solution.py:77
  274.5 7.5 %collective-permute-start.20 = (f32[1,256,4]{2,1,0:T(8,128)S(1)}, f32[1,256,4]{2,1,0:T(8,128)S(1)}, u32[]{:S(2)}, u32[]{:S(2)}) collective-permute-start(f32[1,256,4]{2,1,0:T(8,128)S(1)} %get-tuple-element.108), channel_id=1, source_target_pairs={{8,0},{16,8},{24,16},{32,24},{40,32},{48,40},{56,48},{64,56},{72,6... | collective-permute-start | bytes 12296 | tf_op jit(solution)/shard_map/ppermute | solution.py:24
  282.1 1.9 collective-permute-start.22
  284.3 7.7 %collective-permute-start.23 = (f32[1,256,4]{2,1,0:T(8,128)S(1)}, f32[1,256,4]{2,1,0:T(8,128)S(1)}, u32[]{:S(2)}, u32[]{:S(2)}) collective-permute-start(f32[1,256,4]{2,1,0:T(8,128)S(1)} %get-tuple-element.122), channel_id=1, source_target_pairs={{8,0},{16,8},{24,16},{32,24},{40,32},{48,40},{56,48},{64,56},{72,6... | collective-permute-start | bytes 12296 | tf_op jit(solution)/shard_map/ppermute | solution.py:24
  292.2 6.9 %multiply_subtract_fusion.17 = (f32[256,256]{1,0:T(8,128)S(1)}, f32[256,256]{1,0:T(8,128)S(1)}, f32[256,256]{1,0:T(8,128)S(1)}, f32[256,256]{1,0:T(8,128)S(1)}, ...) fusion(f32[]{:T(128)} %bitcast.12, ...), kind=kLoop, calls=%fused_computation.39 | loop fusion | flops 13893632 | bytes 4993032 | tf_op jit(solution)/shard_map/sub | solution.py:77
  304.0 7.0 %subtract_bitcast_fusion.3 = (f32[1,256,256]{2,1,0:T(8,128)S(1)}, f32[256,256]{1,0:T(8,128)S(1)}, f32[256,256]{1,0:T(8,128)S(1)}, f32[256,256]{1,0:T(8,128)S(1)}...) fusion(f32[]{:T(128)} %bitcast.16, ...), kind=kLoop, calls=%fused_computation.35 | loop fusion | flops 13893632 | bytes 4993032 | tf_op jit(solution)/shard_map/stack | solution.py:104
  (78 shorter events, 44.6 us)
Async XLA Ops:
  7.2 153.6 %all-reduce.11.cloned.1.call-start = ((), (), s32[]{:S(2)}) async-start(), calls=%async_computation | async-start | bytes 4194304 | tf_op jit(solution)/shard_map/psum | solution.py:31
  160.8 16.0 %collective-permute-start = (f32[1,256,256]{2,1,0:T(8,128)}, f32[1,256,256]{2,1,0:T(8,128)S(1)}, u32[]{:S(2)}, u32[]{:S(2)}) collective-permute-start(f32[1,256,256]{2,1,0:T(8,128)} %get-tuple-element.14), channel_id=1, source_target_pairs={{0,384},{8,392},{16,400},{24,408},{32,416},{40,424},{48,432},{56,4... | collective-permute-start | bytes 786440 | tf_op jit(solution)/shard_map/ppermute | solution.py:12
  166.1 17.2 %collective-permute-start.6 = (f32[1,256,256]{2,1,0:T(8,128)}, f32[1,256,256]{2,1,0:T(8,128)S(1)}, u32[]{:S(2)}, u32[]{:S(2)}) collective-permute-start(f32[1,256,256]{2,1,0:T(8,128)} %get-tuple-element.16), channel_id=1, source_target_pairs={{0,384},{8,392},{16,400},{24,408},{32,416},{40,424},{48,432},{56,4... | collective-permute-start | bytes 786440 | tf_op jit(solution)/shard_map/ppermute | solution.py:12
  168.0 20.9 %collective-permute-start.9 = (f32[1,256,256]{2,1,0:T(8,128)}, f32[1,256,256]{2,1,0:T(8,128)S(1)}, u32[]{:S(2)}, u32[]{:S(2)}) collective-permute-start(f32[1,256,256]{2,1,0:T(8,128)} %get-tuple-element.17), channel_id=1, source_target_pairs={{0,384},{8,392},{16,400},{24,408},{32,416},{40,424},{48,432},{56,4... | collective-permute-start | bytes 786440 | tf_op jit(solution)/shard_map/ppermute | solution.py:12
  174.8 19.7 %collective-permute-start.12 = (f32[1,256,256]{2,1,0:T(8,128)}, f32[1,256,256]{2,1,0:T(8,128)S(1)}, u32[]{:S(2)}, u32[]{:S(2)}) collective-permute-start(f32[1,256,256]{2,1,0:T(8,128)} %get-tuple-element.18), channel_id=1, source_target_pairs={{0,384},{8,392},{16,400},{24,408},{32,416},{40,424},{48,432},{56,4... | collective-permute-start | bytes 786440 | tf_op jit(solution)/shard_map/ppermute | solution.py:12
  176.8 24.7 %collective-permute-start.15 = (f32[1,256,256]{2,1,0:T(8,128)}, f32[1,256,256]{2,1,0:T(8,128)S(1)}, u32[]{:S(2)}, u32[]{:S(2)}) collective-permute-start(f32[1,256,256]{2,1,0:T(8,128)} %get-tuple-element.19), channel_id=1, source_target_pairs={{0,384},{8,392},{16,400},{24,408},{32,416},{40,424},{48,432},{56,4... | collective-permute-start | bytes 786440 | tf_op jit(solution)/shard_map/ppermute | solution.py:12
  179.0 29.0 %collective-permute-start.18 = (f32[1,256,256]{2,1,0:T(8,128)S(1)}, f32[1,256,256]{2,1,0:T(8,128)S(1)}, u32[]{:S(2)}, u32[]{:S(2)}) collective-permute-start(f32[1,256,256]{2,1,0:T(8,128)S(1)} %copy-done.5), channel_id=1, source_target_pairs={{0,384},{8,392},{16,400},{24,408},{32,416},{40,424},{48,432},{56,4... | collective-permute-start | bytes 786440 | tf_op jit(solution)/shard_map/ppermute | solution.py:12
  183.3 28.9 %collective-permute-start.21 = (f32[1,256,256]{2,1,0:T(8,128)S(1)}, f32[1,256,256]{2,1,0:T(8,128)S(1)}, u32[]{:S(2)}, u32[]{:S(2)}) collective-permute-start(f32[1,256,256]{2,1,0:T(8,128)S(1)} %copy-done.4), channel_id=1, source_target_pairs={{0,384},{8,392},{16,400},{24,408},{32,416},{40,424},{48,432},{56,4... | collective-permute-start | bytes 786440 | tf_op jit(solution)/shard_map/ppermute | solution.py:12
  188.9 25.3 %collective-permute-start.1 = (f32[1,256,4]{2,1,0:T(8,128)S(1)}, f32[1,256,4]{2,1,0:T(8,128)S(1)}, u32[]{:S(2)}, u32[]{:S(2)}) collective-permute-start(f32[1,256,4]{2,1,0:T(8,128)S(1)} %get-tuple-element.113), channel_id=1, source_target_pairs={{0,8},{8,16},{16,24},{24,32},{32,40},{40,48},{48,56},{56,64},{64,7... | collective-permute-start | bytes 12296 | tf_op jit(solution)/shard_map/ppermute | solution.py:21
  194.5 27.3 %collective-permute-start.2 = (f32[1,256,4]{2,1,0:T(8,128)S(1)}, f32[1,256,4]{2,1,0:T(8,128)S(1)}, u32[]{:S(2)}, u32[]{:S(2)}) collective-permute-start(f32[1,256,4]{2,1,0:T(8,128)S(1)} %get-tuple-element.114), channel_id=1, source_target_pairs={{8,0},{16,8},{24,16},{32,24},{40,32},{48,40},{56,48},{64,56},{72,6... | collective-permute-start | bytes 12296 | tf_op jit(solution)/shard_map/ppermute | solution.py:24
  201.5 22.4 %collective-permute-start.4 = (f32[1,256,4]{2,1,0:T(8,128)S(1)}, f32[1,256,4]{2,1,0:T(8,128)S(1)}, u32[]{:S(2)}, u32[]{:S(2)}) collective-permute-start(f32[1,256,4]{2,1,0:T(8,128)S(1)} %get-tuple-element.115), channel_id=1, source_target_pairs={{0,8},{8,16},{16,24},{24,32},{32,40},{40,48},{48,56},{56,64},{64,7... | collective-permute-start | bytes 12296 | tf_op jit(solution)/shard_map/ppermute | solution.py:21
  208.0 23.5 %collective-permute-start.5 = (f32[1,256,4]{2,1,0:T(8,128)S(1)}, f32[1,256,4]{2,1,0:T(8,128)S(1)}, u32[]{:S(2)}, u32[]{:S(2)}) collective-permute-start(f32[1,256,4]{2,1,0:T(8,128)S(1)} %get-tuple-element.116), channel_id=1, source_target_pairs={{8,0},{16,8},{24,16},{32,24},{40,32},{48,40},{56,48},{64,56},{72,6... | collective-permute-start | bytes 12296 | tf_op jit(solution)/shard_map/ppermute | solution.py:24
  212.2 31.7 %collective-permute-start.7 = (f32[1,256,4]{2,1,0:T(8,128)S(1)}, f32[1,256,4]{2,1,0:T(8,128)S(1)}, u32[]{:S(2)}, u32[]{:S(2)}) collective-permute-start(f32[1,256,4]{2,1,0:T(8,128)S(1)} %get-tuple-element.111), channel_id=1, source_target_pairs={{0,8},{8,16},{16,24},{24,32},{32,40},{40,48},{48,56},{56,64},{64,7... | collective-permute-start | bytes 12296 | tf_op jit(solution)/shard_map/ppermute | solution.py:21
  214.2 37.2 %collective-permute-start.8 = (f32[1,256,4]{2,1,0:T(8,128)S(1)}, f32[1,256,4]{2,1,0:T(8,128)S(1)}, u32[]{:S(2)}, u32[]{:S(2)}) collective-permute-start(f32[1,256,4]{2,1,0:T(8,128)S(1)} %get-tuple-element.112), channel_id=1, source_target_pairs={{8,0},{16,8},{24,16},{32,24},{40,32},{48,40},{56,48},{64,56},{72,6... | collective-permute-start | bytes 12296 | tf_op jit(solution)/shard_map/ppermute | solution.py:24
  221.8 31.8 %collective-permute-start.10 = (f32[1,256,4]{2,1,0:T(8,128)S(1)}, f32[1,256,4]{2,1,0:T(8,128)S(1)}, u32[]{:S(2)}, u32[]{:S(2)}) collective-permute-start(f32[1,256,4]{2,1,0:T(8,128)S(1)} %get-tuple-element.117), channel_id=1, source_target_pairs={{0,8},{8,16},{16,24},{24,32},{32,40},{40,48},{48,56},{56,64},{64,7... | collective-permute-start | bytes 12296 | tf_op jit(solution)/shard_map/ppermute | solution.py:21
  224.0 37.2 %collective-permute-start.11 = (f32[1,256,4]{2,1,0:T(8,128)S(1)}, f32[1,256,4]{2,1,0:T(8,128)S(1)}, u32[]{:S(2)}, u32[]{:S(2)}) collective-permute-start(f32[1,256,4]{2,1,0:T(8,128)S(1)} %get-tuple-element.118), channel_id=1, source_target_pairs={{8,0},{16,8},{24,16},{32,24},{40,32},{48,40},{56,48},{64,56},{72,6... | collective-permute-start | bytes 12296 | tf_op jit(solution)/shard_map/ppermute | solution.py:24
  231.5 43.0 %collective-permute-start.13 = (f32[1,256,4]{2,1,0:T(8,128)S(1)}, f32[1,256,4]{2,1,0:T(8,128)S(1)}, u32[]{:S(2)}, u32[]{:S(2)}) collective-permute-start(f32[1,256,4]{2,1,0:T(8,128)S(1)} %get-tuple-element.109), channel_id=1, source_target_pairs={{0,8},{8,16},{16,24},{24,32},{32,40},{40,48},{48,56},{56,64},{64,7... | collective-permute-start | bytes 12296 | tf_op jit(solution)/shard_map/ppermute | solution.py:21
  243.9 38.2 %collective-permute-start.14 = (f32[1,256,4]{2,1,0:T(8,128)S(1)}, f32[1,256,4]{2,1,0:T(8,128)S(1)}, u32[]{:S(2)}, u32[]{:S(2)}) collective-permute-start(f32[1,256,4]{2,1,0:T(8,128)S(1)} %get-tuple-element.110), channel_id=1, source_target_pairs={{8,0},{16,8},{24,16},{32,24},{40,32},{48,40},{56,48},{64,56},{72,6... | collective-permute-start | bytes 12296 | tf_op jit(solution)/shard_map/ppermute | solution.py:24
  251.4 32.8 %collective-permute-start.16 = (f32[1,256,4]{2,1,0:T(8,128)S(1)}, f32[1,256,4]{2,1,0:T(8,128)S(1)}, u32[]{:S(2)}, u32[]{:S(2)}) collective-permute-start(f32[1,256,4]{2,1,0:T(8,128)S(1)} %get-tuple-element.119), channel_id=1, source_target_pairs={{0,8},{8,16},{16,24},{24,32},{32,40},{40,48},{48,56},{56,64},{64,7... | collective-permute-start | bytes 12296 | tf_op jit(solution)/shard_map/ppermute | solution.py:21
  253.6 38.4 %collective-permute-start.17 = (f32[1,256,4]{2,1,0:T(8,128)S(1)}, f32[1,256,4]{2,1,0:T(8,128)S(1)}, u32[]{:S(2)}, u32[]{:S(2)}) collective-permute-start(f32[1,256,4]{2,1,0:T(8,128)S(1)} %get-tuple-element.120), channel_id=1, source_target_pairs={{8,0},{16,8},{24,16},{32,24},{40,32},{48,40},{56,48},{64,56},{72,6... | collective-permute-start | bytes 12296 | tf_op jit(solution)/shard_map/ppermute | solution.py:24
  261.2 42.4 %collective-permute-start.19 = (f32[1,256,4]{2,1,0:T(8,128)S(1)}, f32[1,256,4]{2,1,0:T(8,128)S(1)}, u32[]{:S(2)}, u32[]{:S(2)}) collective-permute-start(f32[1,256,4]{2,1,0:T(8,128)S(1)} %get-tuple-element.107), channel_id=1, source_target_pairs={{0,8},{8,16},{16,24},{24,32},{32,40},{40,48},{48,56},{56,64},{64,7... | collective-permute-start | bytes 12296 | tf_op jit(solution)/shard_map/ppermute | solution.py:21
  274.5 29.0 %collective-permute-start.20 = (f32[1,256,4]{2,1,0:T(8,128)S(1)}, f32[1,256,4]{2,1,0:T(8,128)S(1)}, u32[]{:S(2)}, u32[]{:S(2)}) collective-permute-start(f32[1,256,4]{2,1,0:T(8,128)S(1)} %get-tuple-element.108), channel_id=1, source_target_pairs={{8,0},{16,8},{24,16},{32,24},{40,32},{48,40},{56,48},{64,56},{72,6... | collective-permute-start | bytes 12296 | tf_op jit(solution)/shard_map/ppermute | solution.py:24
  282.1 21.7 %collective-permute-start.22 = (f32[1,256,4]{2,1,0:T(8,128)S(1)}, f32[1,256,4]{2,1,0:T(8,128)S(1)}, u32[]{:S(2)}, u32[]{:S(2)}) collective-permute-start(f32[1,256,4]{2,1,0:T(8,128)S(1)} %get-tuple-element.121), channel_id=1, source_target_pairs={{0,8},{8,16},{16,24},{24,32},{32,40},{40,48},{48,56},{56,64},{64,7... | collective-permute-start | bytes 12296 | tf_op jit(solution)/shard_map/ppermute | solution.py:21
  284.3 19.5 %collective-permute-start.23 = (f32[1,256,4]{2,1,0:T(8,128)S(1)}, f32[1,256,4]{2,1,0:T(8,128)S(1)}, u32[]{:S(2)}, u32[]{:S(2)}) collective-permute-start(f32[1,256,4]{2,1,0:T(8,128)S(1)} %get-tuple-element.122), channel_id=1, source_target_pairs={{8,0},{16,8},{24,16},{32,24},{40,32},{48,40},{56,48},{64,56},{72,6... | collective-permute-start | bytes 12296 | tf_op jit(solution)/shard_map/ppermute | solution.py:24
  (7 other events, 26.0 us)
Sparse Core Ops, SparseCore 0:
  12.1 148.6 all-reduce.10
where the time goes:
time: 325 us; the launch traced here: 324 us
  waiting for transfers between devices  165 us (51%)
  starting transfers between devices  91.6 us (28%)
  other arithmetic  50.1 us (15%)
  between operations  14.6 us (4%)
  local copies, waits for them, and re-layouts  3.43 us (1%)
    psum x1, waiting for transfers between devices, from_root(): return lax.psum(jnp.where(mine, shard, jnp.zeros_like(shard)), axis)  150 us
    ppermute x8, starting transfers between devices, extended(): lax.ppermute(lax.slice_in_dim(block, 0, width, axis=dim), axis, backward)  52.5 us
    ppermute x8, starting transfers between devices, shifted(): return lax.ppermute(value, axis, pairs)  23.7 us
    sub x3, other arithmetic, advance(): b_zz = a_zz - gain * (shear_tt * a_zz + shear_tp * a_oz)  20.6 us
    ppermute x8, starting transfers between devices, extended(): lax.ppermute(lax.slice_in_dim(block, block.shape[dim] - width, None, axis...  15.3 us
    ppermute x8, waiting for transfers between devices, shifted(): return lax.ppermute(value, axis, pairs)  14.6 us
    another operation x3, other arithmetic, per_device(): jacobian = jnp.stack(state[2:6])[None]  9.68 us
  transfers between devices with their start and end apart: 25, of which 7 were waited for; matrix products, arithmetic and copies ran while one was open for 11% of the time, Pallas kernels for 0%

commit v1 on v0

--- a/solution.py
+++ b/solution.py
@@ -28,7 +28,7 @@
 
 def from_root(shard, axis, root):
     mine = lax.axis_index(axis) == root
-    return lax.psum(jnp.where(mine, shard, jnp.zeros_like(shard)), axis)
+    return jnp.sum(lax.all_gather(jnp.where(mine, shard, jnp.zeros_like(shard)), axis), axis=0)
 
 
 def pick_cycle(row_block, shifts, offset, width):

time: 325 us -> 809 us (2.49)
  waiting for transfers between devices: 165 us -> 628 us
  other arithmetic: 50.1 us -> 63.6 us
  starting transfers between devices: 91.6 us -> 99.8 us
    all_gather x0 -> x8, waiting for transfers between devices: none -> 624 us  [from_root(): lax.all_gather(jnp.where(mine, shard, jnp.zeros_like(shard)), axis)]
    psum x1 -> x0, waiting for transfers between devices: 150 us -> none  [from_root(): return lax.psum(jnp.where(mine, shard, jnp.zeros_like(shard)), axis)]
    ppermute x8, waiting for transfers between devices: 14.6 us -> 0.02 us  [shifted(): return lax.ppermute(value, axis, pairs)]
    reduce_sum x0 -> x8, other arithmetic: none -> 14 us  [from_root(): jnp.sum(lax.all_gather(jnp.where(mine, shard, jnp.zeros_like(shard)), axi...]
  transfers between devices with their start and end apart: 25 -> 32, of which waited for: 7 -> 8; matrix products, arithmetic and copies ran while one was open for 11% -> 6% of each run, Pallas kernels for 0% -> 0%
where the time goes in v1:
time: 809 us; the launch traced here: 808 us
  waiting for transfers between devices  628 us (78%)
  starting transfers between devices  99.8 us (12%)
  other arithmetic  63.6 us (8%)
  between operations  14.8 us (2%)
    all_gather x8, waiting for transfers between devices, from_root(): lax.all_gather(jnp.where(mine, shard, jnp.zeros_like(shard)), axis)  624 us
    ppermute x8, starting transfers between devices, extended(): lax.ppermute(lax.slice_in_dim(block, 0, width, axis=dim), axis, backward)  60.6 us
    ppermute x8, starting transfers between devices, shifted(): return lax.ppermute(value, axis, pairs)  23.6 us
    sub x3, other arithmetic, advance(): b_zz = a_zz - gain * (shear_tt * a_zz + shear_tp * a_oz)  20.5 us
  transfers between devices with their start and end apart: 32, of which 8 were waited for; matrix products, arithmetic and copies ran while one was open for 6% of the time, Pallas kernels for 0%

profile of v1, /device:TPU:6, one launch (start us, length us, event | category | flops | bytes accessed | tf_op | source)
XLA Modules:
  0.0 807.7 jit_solution(8113719325465175573)
XLA Ops:
  14.3 83.3 %all-gather.19.cloned.1.call-done = f32[8,256,256]{2,1,0:T(8,128)} async-done(((f32[1,256,256]{2,1,0:T(8,128)}), f32[8,256,256]{2,1,0:T(8,128)}) %all-gather.19.cloned.1.call-update) | async-done | bytes 2097168 | tf_op jit(solution)/shard_map/all_gather | solution.py:31
  99.4 2.9 collective-permute-start.3
  102.5 76.3 %all-gather.17.cloned.1.call-done = f32[8,256,256]{2,1,0:T(8,128)} async-done(((f32[1,256,256]{2,1,0:T(8,128)}), f32[8,256,256]{2,1,0:T(8,128)}) %all-gather.17.cloned.1.call-update) | async-done | bytes 2097168 | tf_op jit(solution)/shard_map/all_gather | solution.py:31
  180.5 2.9 collective-permute-start
  184.1 75.7 %all-gather.23.cloned.1.call-done = f32[8,256,256]{2,1,0:T(8,128)} async-done(((f32[1,256,256]{2,1,0:T(8,128)}), f32[8,256,256]{2,1,0:T(8,128)}) %all-gather.23.cloned.1.call-update) | async-done | bytes 2097168 | tf_op jit(solution)/shard_map/all_gather | solution.py:31
  264.5 76.2 %all-gather.21.cloned.1.call-done = f32[8,256,256]{2,1,0:T(8,128)} async-done(((f32[1,256,256]{2,1,0:T(8,128)}), f32[8,256,256]{2,1,0:T(8,128)}) %all-gather.21.cloned.1.call-update) | async-done | bytes 2097168 | tf_op jit(solution)/shard_map/all_gather | solution.py:31
  345.3 76.8 %all-gather.27.cloned.1.call-done = f32[8,256,256]{2,1,0:T(8,128)} async-done(((f32[1,256,256]{2,1,0:T(8,128)}), f32[8,256,256]{2,1,0:T(8,128)}) %all-gather.27.cloned.1.call-update) | async-done | bytes 2097168 | tf_op jit(solution)/shard_map/all_gather | solution.py:31
  426.8 76.2 %all-gather.25.cloned.1.call-done = f32[8,256,256]{2,1,0:T(8,128)} async-done(((f32[1,256,256]{2,1,0:T(8,128)}), f32[8,256,256]{2,1,0:T(8,128)}) %all-gather.25.cloned.1.call-update) | async-done | bytes 2097168 | tf_op jit(solution)/shard_map/all_gather | solution.py:31
  504.8 79.3 %all-gather.31.cloned.1.call-done = f32[8,256,256]{2,1,0:T(8,128)} async-done(((f32[1,256,256]{2,1,0:T(8,128)}), f32[8,256,256]{2,1,0:T(8,128)}) %all-gather.31.cloned.1.call-update) | async-done | bytes 2097168 | tf_op jit(solution)/shard_map/all_gather | solution.py:31
  585.8 79.9 %all-gather.29.cloned.1.call-done = f32[8,256,256]{2,1,0:T(8,128)} async-done(((f32[1,256,256]{2,1,0:T(8,128)}), f32[8,256,256]{2,1,0:T(8,128)}) %all-gather.29.cloned.1.call-update) | async-done | bytes 2097168 | tf_op jit(solution)/shard_map/all_gather | solution.py:31
  667.4 2.9 collective-permute-start.12
  673.2 3.4 collective-permute-start.18
  678.8 7.5 collective-permute-start.5
  688.5 7.5 collective-permute-start.2
  698.2 7.5 collective-permute-start.11
  707.9 7.5 collective-permute-start.8
  717.6 6.8 multiply_subtract_fusion.25
  727.8 7.5 collective-permute-start.17
  737.5 7.5 collective-permute-start.14
  747.2 6.8 multiply_subtract_fusion.21
  758.2 7.5 collective-permute-start.23
  767.9 7.7 collective-permute-start.20
  775.8 6.9 multiply_subtract_fusion.17
  787.6 6.9 subtract_bitcast_fusion.3
  (103 shorter events, 69.1 us)
Async XLA Ops:
  7.2 90.5 %all-gather.19.cloned.1.call-start = ((), (), s32[]{:S(2)}) async-start(), calls=%async_computation.1 | async-start | bytes 2359296 | tf_op jit(solution)/shard_map/all_gather | solution.py:31
  9.6 169.2 %all-gather.17.cloned.1.call-start = ((), (), s32[]{:S(2)}) async-start(), calls=%async_computation | async-start | bytes 2359296 | tf_op jit(solution)/shard_map/all_gather | solution.py:31
  10.3 249.5 %all-gather.23.cloned.1.call-start = ((), (), s32[]{:S(2)}) async-start(), calls=%async_computation.3 | async-start | bytes 2359296 | tf_op jit(solution)/shard_map/all_gather | solution.py:31
  11.0 329.6 %all-gather.21.cloned.1.call-start = ((), (), s32[]{:S(2)}) async-start(), calls=%async_computation.2 | async-start | bytes 2359296 | tf_op jit(solution)/shard_map/all_gather | solution.py:31
  11.6 410.5 %all-gather.27.cloned.1.call-start = ((), (), s32[]{:S(2)}) async-start(), calls=%async_computation.5 | async-start | bytes 2359296 | tf_op jit(solution)/shard_map/all_gather | solution.py:31
  12.2 490.8 %all-gather.25.cloned.1.call-start = ((), (), s32[]{:S(2)}) async-start(), calls=%async_computation.4 | async-start | bytes 2359296 | tf_op jit(solution)/shard_map/all_gather | solution.py:31
  12.8 571.3 %all-gather.31.cloned.1.call-start = ((), (), s32[]{:S(2)}) async-start(), calls=%async_computation.7 | async-start | bytes 2359296 | tf_op jit(solution)/shard_map/all_gather | solution.py:31
  13.5 652.1 %all-gather.29.cloned.1.call-start = ((), (), s32[]{:S(2)}) async-start(), calls=%async_computation.6 | async-start | bytes 2359296 | tf_op jit(solution)/shard_map/all_gather | solution.py:31
  99.4 568.0 %collective-permute-start.3 = (f32[1,256,256]{2,1,0:T(8,128)S(1)}, f32[1,256,256]{2,1,0:T(8,128)S(1)}, u32[]{:S(2)}, u32[]{:S(2)}) collective-permute-start(f32[1,256,256]{2,1,0:T(8,128)S(1)} %bitcast.50), channel_id=1, source_target_pairs={{0,384},{8,392},{16,400},{24,408},{32,416},{40,424},{48,432},{56,4... | collective-permute-start | bytes 786440 | tf_op jit(solution)/shard_map/ppermute | solution.py:12
  180.5 490.0 %collective-permute-start = (f32[1,256,256]{2,1,0:T(8,128)S(1)}, f32[1,256,256]{2,1,0:T(8,128)S(1)}, u32[]{:S(2)}, u32[]{:S(2)}) collective-permute-start(f32[1,256,256]{2,1,0:T(8,128)S(1)} %bitcast.53), channel_id=1, source_target_pairs={{0,384},{8,392},{16,400},{24,408},{32,416},{40,424},{48,432},{56,4... | collective-permute-start | bytes 786440 | tf_op jit(solution)/shard_map/ppermute | solution.py:12
  261.5 411.7 %collective-permute-start.9 = (f32[1,256,256]{2,1,0:T(8,128)S(1)}, f32[1,256,256]{2,1,0:T(8,128)S(1)}, u32[]{:S(2)}, u32[]{:S(2)}) collective-permute-start(f32[1,256,256]{2,1,0:T(8,128)S(1)} %bitcast.57), channel_id=1, source_target_pairs={{0,384},{8,392},{16,400},{24,408},{32,416},{40,424},{48,432},{56,4... | collective-permute-start | bytes 786440 | tf_op jit(solution)/shard_map/ppermute | solution.py:12
  342.4 334.3 %collective-permute-start.6 = (f32[1,256,256]{2,1,0:T(8,128)S(1)}, f32[1,256,256]{2,1,0:T(8,128)S(1)}, u32[]{:S(2)}, u32[]{:S(2)}) collective-permute-start(f32[1,256,256]{2,1,0:T(8,128)S(1)} %bitcast.56), channel_id=1, source_target_pairs={{0,384},{8,392},{16,400},{24,408},{32,416},{40,424},{48,432},{56,4... | collective-permute-start | bytes 786440 | tf_op jit(solution)/shard_map/ppermute | solution.py:12
  423.9 254.9 %collective-permute-start.15 = (f32[1,256,256]{2,1,0:T(8,128)S(1)}, f32[1,256,256]{2,1,0:T(8,128)S(1)}, u32[]{:S(2)}, u32[]{:S(2)}) collective-permute-start(f32[1,256,256]{2,1,0:T(8,128)S(1)} %bitcast.55), channel_id=1, source_target_pairs={{0,384},{8,392},{16,400},{24,408},{32,416},{40,424},{48,432},{56,4... | collective-permute-start | bytes 786440 | tf_op jit(solution)/shard_map/ppermute | solution.py:12
  688.5 27.0 %collective-permute-start.2 = (f32[1,256,4]{2,1,0:T(8,128)S(1)}, f32[1,256,4]{2,1,0:T(8,128)S(1)}, u32[]{:S(2)}, u32[]{:S(2)}) collective-permute-start(f32[1,256,4]{2,1,0:T(8,128)S(1)} %get-tuple-element.114), channel_id=1, source_target_pairs={{8,0},{16,8},{24,16},{32,24},{40,32},{48,40},{56,48},{64,56},{72,6... | collective-permute-start | bytes 12296 | tf_op jit(solution)/shard_map/ppermute | solution.py:24
  696.1 31.7 %collective-permute-start.10 = (f32[1,256,4]{2,1,0:T(8,128)S(1)}, f32[1,256,4]{2,1,0:T(8,128)S(1)}, u32[]{:S(2)}, u32[]{:S(2)}) collective-permute-start(f32[1,256,4]{2,1,0:T(8,128)S(1)} %get-tuple-element.117), channel_id=1, source_target_pairs={{0,8},{8,16},{16,24},{24,32},{32,40},{40,48},{48,56},{56,64},{64,7... | collective-permute-start | bytes 12296 | tf_op jit(solution)/shard_map/ppermute | solution.py:21
  698.2 37.2 %collective-permute-start.11 = (f32[1,256,4]{2,1,0:T(8,128)S(1)}, f32[1,256,4]{2,1,0:T(8,128)S(1)}, u32[]{:S(2)}, u32[]{:S(2)}) collective-permute-start(f32[1,256,4]{2,1,0:T(8,128)S(1)} %get-tuple-element.118), channel_id=1, source_target_pairs={{8,0},{16,8},{24,16},{32,24},{40,32},{48,40},{56,48},{64,56},{72,6... | collective-permute-start | bytes 12296 | tf_op jit(solution)/shard_map/ppermute | solution.py:24
  705.7 31.8 %collective-permute-start.7 = (f32[1,256,4]{2,1,0:T(8,128)S(1)}, f32[1,256,4]{2,1,0:T(8,128)S(1)}, u32[]{:S(2)}, u32[]{:S(2)}) collective-permute-start(f32[1,256,4]{2,1,0:T(8,128)S(1)} %get-tuple-element.111), channel_id=1, source_target_pairs={{0,8},{8,16},{16,24},{24,32},{32,40},{40,48},{48,56},{56,64},{64,7... | collective-permute-start | bytes 12296 | tf_op jit(solution)/shard_map/ppermute | solution.py:21
  707.9 37.2 %collective-permute-start.8 = (f32[1,256,4]{2,1,0:T(8,128)S(1)}, f32[1,256,4]{2,1,0:T(8,128)S(1)}, u32[]{:S(2)}, u32[]{:S(2)}) collective-permute-start(f32[1,256,4]{2,1,0:T(8,128)S(1)} %get-tuple-element.112), channel_id=1, source_target_pairs={{8,0},{16,8},{24,16},{32,24},{40,32},{48,40},{56,48},{64,56},{72,6... | collective-permute-start | bytes 12296 | tf_op jit(solution)/shard_map/ppermute | solution.py:24
  715.4 42.7 %collective-permute-start.16 = (f32[1,256,4]{2,1,0:T(8,128)S(1)}, f32[1,256,4]{2,1,0:T(8,128)S(1)}, u32[]{:S(2)}, u32[]{:S(2)}) collective-permute-start(f32[1,256,4]{2,1,0:T(8,128)S(1)} %get-tuple-element.119), channel_id=1, source_target_pairs={{0,8},{8,16},{16,24},{24,32},{32,40},{40,48},{48,56},{56,64},{64,7... | collective-permute-start | bytes 12296 | tf_op jit(solution)/shard_map/ppermute | solution.py:21
  727.8 37.9 %collective-permute-start.17 = (f32[1,256,4]{2,1,0:T(8,128)S(1)}, f32[1,256,4]{2,1,0:T(8,128)S(1)}, u32[]{:S(2)}, u32[]{:S(2)}) collective-permute-start(f32[1,256,4]{2,1,0:T(8,128)S(1)} %get-tuple-element.120), channel_id=1, source_target_pairs={{8,0},{16,8},{24,16},{32,24},{40,32},{48,40},{56,48},{64,56},{72,6... | collective-permute-start | bytes 12296 | tf_op jit(solution)/shard_map/ppermute | solution.py:24
  735.4 32.5 %collective-permute-start.13 = (f32[1,256,4]{2,1,0:T(8,128)S(1)}, f32[1,256,4]{2,1,0:T(8,128)S(1)}, u32[]{:S(2)}, u32[]{:S(2)}) collective-permute-start(f32[1,256,4]{2,1,0:T(8,128)S(1)} %get-tuple-element.109), channel_id=1, source_target_pairs={{0,8},{8,16},{16,24},{24,32},{32,40},{40,48},{48,56},{56,64},{64,7... | collective-permute-start | bytes 12296 | tf_op jit(solution)/shard_map/ppermute | solution.py:21
  737.5 38.1 %collective-permute-start.14 = (f32[1,256,4]{2,1,0:T(8,128)S(1)}, f32[1,256,4]{2,1,0:T(8,128)S(1)}, u32[]{:S(2)}, u32[]{:S(2)}) collective-permute-start(f32[1,256,4]{2,1,0:T(8,128)S(1)} %get-tuple-element.110), channel_id=1, source_target_pairs={{8,0},{16,8},{24,16},{32,24},{40,32},{48,40},{56,48},{64,56},{72,6... | collective-permute-start | bytes 12296 | tf_op jit(solution)/shard_map/ppermute | solution.py:24
  745.1 42.1 %collective-permute-start.22 = (f32[1,256,4]{2,1,0:T(8,128)S(1)}, f32[1,256,4]{2,1,0:T(8,128)S(1)}, u32[]{:S(2)}, u32[]{:S(2)}) collective-permute-start(f32[1,256,4]{2,1,0:T(8,128)S(1)} %get-tuple-element.121), channel_id=1, source_target_pairs={{0,8},{8,16},{16,24},{24,32},{32,40},{40,48},{48,56},{56,64},{64,7... | collective-permute-start | bytes 12296 | tf_op jit(solution)/shard_map/ppermute | solution.py:21
  758.2 29.0 %collective-permute-start.23 = (f32[1,256,4]{2,1,0:T(8,128)S(1)}, f32[1,256,4]{2,1,0:T(8,128)S(1)}, u32[]{:S(2)}, u32[]{:S(2)}) collective-permute-start(f32[1,256,4]{2,1,0:T(8,128)S(1)} %get-tuple-element.122), channel_id=1, source_target_pairs={{8,0},{16,8},{24,16},{32,24},{40,32},{48,40},{56,48},{64,56},{72,6... | collective-permute-start | bytes 12296 | tf_op jit(solution)/shard_map/ppermute | solution.py:24
  (12 other events, 446.8 us)
Sparse Core Ops, SparseCore 0:
  11.2 86.4 all-gather.18
  100.9 77.7 all-gather.16
  181.9 77.7 all-gather.22
  262.8 77.7 all-gather.20
  344.3 77.7 all-gather.26
  425.2 77.7 all-gather.24
  506.2 77.7 all-gather.30
  587.8 77.7 all-gather.28
